TPU v7x, 32 devices: a whole 2x2x4 slice. The times are simulated.
32 devices in a mesh: groups: 2 (over y), img: 4 (over z), pair: 2 (over x), sub: 2 (over core).
Axes of the slice: x: 2, y: 2, z: 4, core: 2. Of those that a mesh axis runs over, the one named last changes fastest.
Arguments:
- descriptors: bfloat16 [16, 1024, 256], P(('groups', 'img', 'pair')), parts along dimension 0
- links: int32 [16, 3], P('groups'), parts along dimension 0, may hold values 0 or 1
- qk_weight: bfloat16 [256, 256], P(None, 'sub'), may hold values from -0.375 to 0.375
- value_weight: bfloat16 [256, 256], P(None, 'sub'), may hold values from -0.375 to 0.375
- out_weight: bfloat16 [256, 256], replicated, may hold values from -0.375 to 0.375
- mlp_in: bfloat16 [512, 512], replicated, may hold values from -0.25 to 0.25
- mlp_in_bias: float32 [512], replicated, may hold values from -4 to 4
- norm_gain: float32 [512], replicated, may hold values from 0.1 to 1.9
- norm_bias: float32 [512], replicated, may hold values from -3 to 3
- mlp_out: bfloat16 [512, 256], replicated, may hold values from -0.25 to 0.25
- mlp_out_bias: float32 [256], replicated, may hold values from -3 to 3
Outputs:
- updated: bfloat16 [16, 1024, 256], P(('groups', 'img', 'pair'), 'sub'), parts along dimension 0
There are 2 independent parts, one for each index of `groups`. A program takes and returns all parts, laid end to end along the dimension named above; an argument that names none is the same for every part. Nothing has to cross between parts.
All inputs are finite; a program needn't handle non-finite values.
Results may differ from a plain program's by a relative error of at most 0.0045.
Values may be sent and summed in bfloat16 or wider, within the bound.
No kernel may reach another device: no remote copies, remote signals or barrier semaphores. Data moves between devices by JAX's collectives and lax.ppermute only.
A program may use at most 64 MiB of HBM per device.

v0:
```python
import math
import jax
import jax.numpy as jnp
from jax import lax
from jax.sharding import PartitionSpec as P

D = 256
HEADS = 4
SPAN = 3


def passed_along(value, axis, by):
    length = lax.axis_size(axis)
    pairs = [(i, i + by) for i in range(length) if 0 <= i + by < length]
    return lax.ppermute(value, axis, pairs)


def link_value(links, lower_image, step_size, image_count):
    inside = jnp.logical_and(lower_image >= 0, lower_image + step_size < image_count)
    clipped = jnp.clip(lower_image, 0, image_count - 1)
    entry = lax.dynamic_slice(links, (clipped, jnp.int32(step_size - 1)), (1, 1))[0, 0]
    return jnp.where(inside, entry, 0).astype(jnp.float32)


def fetch_partner(offset, packed, local_width):
    partner = passed_along(packed, ("img", "pair"), -offset)
    return (partner[:, :local_width], partner[:, local_width:])


def tile_messages(own_keys, partner_keys, partner_values):
    head_width = D // HEADS
    score_scale = 1.0 / math.sqrt(head_width)
    heads_local = own_keys.shape[1] // head_width
    to_own = []
    for head_id in range(heads_local):
        lo_col = head_id * head_width
        query_part = own_keys[:, lo_col : lo_col + head_width]
        key_part = partner_keys[:, lo_col : lo_col + head_width]
        scores = (
            jnp.einsum("qd,kd->qk", query_part, key_part, preferred_element_type=jnp.float32)
            * score_scale
        )
        row_weights = jax.nn.softmax(scores, axis=1).astype(jnp.bfloat16)
        to_own.append(
            jnp.dot(
                row_weights,
                partner_values[:, lo_col : lo_col + head_width],
                preferred_element_type=jnp.float32,
            ).astype(jnp.bfloat16)
        )
    own_result = jnp.concatenate(to_own, axis=1)
    return (own_result, own_result)


def on_device(
    descriptors,
    links,
    qk_weight,
    value_weight,
    out_weight,
    mlp_in,
    mlp_in_bias,
    norm_gain,
    norm_bias,
    mlp_out,
    mlp_out_bias,
):
    own_rows = descriptors[0]
    key_rows = jnp.dot(own_rows, qk_weight, preferred_element_type=jnp.float32).astype(jnp.bfloat16)
    value_rows = jnp.dot(own_rows, value_weight, preferred_element_type=jnp.float32).astype(
        jnp.bfloat16
    )
    local_width = key_rows.shape[1]
    packed = jnp.concatenate([key_rows, value_rows], axis=1)
    half_rows = own_rows.shape[0] // lax.axis_size("sub")
    row_start = lax.axis_index("sub") * half_rows
    own_half = lax.dynamic_slice_in_dim(own_rows, row_start, half_rows, 0)
    position = lax.axis_index(("img", "pair"))
    image_count = lax.axis_size(("img", "pair"))
    summed = jnp.zeros(key_rows.shape, jnp.float32)
    offsets = list(range(1, SPAN + 1)) + list(range(-SPAN, 0))
    for offset in offsets:
        partner_keys, partner_values = fetch_partner(offset, packed, local_width)
        step_size = abs(offset)
        lower_image = position + min(offset, 0)
        linked = link_value(links, lower_image, step_size, image_count)
        message, unused = tile_messages(key_rows, partner_keys, partner_values)
        summed = summed + linked * message.astype(jnp.float32)
    summed_b = summed.astype(jnp.bfloat16)
    gathered = lax.all_to_all(summed_b, "sub", split_axis=0, concat_axis=1, tiled=True)
    projected = jnp.dot(gathered, out_weight, preferred_element_type=jnp.float32).astype(
        jnp.bfloat16
    )
    hidden = jnp.dot(own_half, mlp_in[:D], preferred_element_type=jnp.float32)
    hidden = (
        hidden + jnp.dot(projected, mlp_in[D:], preferred_element_type=jnp.float32) + mlp_in_bias
    )
    mean_value = jnp.mean(hidden, axis=1, keepdims=True)
    centered = hidden - mean_value
    variance = jnp.mean(centered * centered, axis=1, keepdims=True)
    normed = centered * lax.rsqrt(variance + 1e-05) * norm_gain + norm_bias
    activated = jax.nn.gelu(normed, approximate=False).astype(jnp.bfloat16)
    output_rows = jnp.dot(activated, mlp_out, preferred_element_type=jnp.float32) + mlp_out_bias
    output_rows = output_rows + own_half.astype(jnp.float32)
    return output_rows.astype(jnp.bfloat16)[None]


def solution(mesh):
    placed = (
        P(("groups", "img", "pair"), None, None),
        P("groups", None),
        P(None, "sub"),
        P(None, "sub"),
        P(),
        P(),
        P(),
        P(),
        P(),
        P(),
        P(),
    )
    return jax.shard_map(
        on_device,
        mesh=mesh,
        in_specs=placed,
        out_specs=P(("groups", "img", "pair"), "sub", None),
        check_vma=False,
    )
```

profile of v0, /device:TPU:17, one launch (start us, length us, event | category | flops | bytes accessed | tf_op | source)
XLA Modules:
  0.0 95.1 jit_solution(5887512537064446653)
XLA Ops:
  0.0 1.4 %convolution_convert_fusion.2 = bf16[1024,128]{0,1:T(8,128)(2,1)S(1)} fusion(bf16[256,128]{1,0:T(8,128)(2,1)} %param.13, bf16[1,1024,256]{2,1,0:T(8,128)(2,1)} %param.11), kind=kOutput, calls=%fused_computation.68 | convolution fusion | flops 67239936 | bytes 851968 | tf_op jit(solution)/shard_map/dot_general | solution.py:69
  2.8 3.1 %collective-permute-start.5 = (bf16[1024,256]{0,1:T(8,128)(2,1)S(1)}, bf16[1024,256]{0,1:T(8,128)(2,1)}, u32[]{:S(2)}, u32[]{:S(2)}) collective-permute-start(bf16[1024,256]{0,1:T(8,128)(2,1)S(1)} %pad_maximum_fusion), channel_id=1, source_target_pairs={{0,2},{2,4},{4,6},{6,8},{8,10},{10,12},{12,14},{1,3},{3,5},{5,7},{... | collective-permute-start | bytes 1572872 | tf_op jit(solution)/shard_map/ppermute | solution.py:15
  5.9 3.2 %collective-permute-start.4 = (bf16[1024,256]{0,1:T(8,128)(2,1)S(1)}, bf16[1024,256]{0,1:T(8,128)(2,1)}, u32[]{:S(2)}, u32[]{:S(2)}) collective-permute-start(bf16[1024,256]{0,1:T(8,128)(2,1)S(1)} %pad_maximum_fusion), channel_id=1, source_target_pairs={{0,4},{2,6},{4,8},{6,10},{8,12},{10,14},{1,5},{3,7},{5,9},{7,11},{... | collective-permute-start | bytes 1572872 | tf_op jit(solution)/shard_map/ppermute | solution.py:15
  9.1 1.9 %collective-permute-start.3 = (bf16[1024,256]{0,1:T(8,128)(2,1)S(1)}, bf16[1024,256]{0,1:T(8,128)(2,1)}, u32[]{:S(2)}, u32[]{:S(2)}) collective-permute-start(bf16[1024,256]{0,1:T(8,128)(2,1)S(1)} %pad_maximum_fusion), channel_id=1, source_target_pairs={{0,6},{2,8},{4,10},{6,12},{8,14},{1,7},{3,9},{5,11},{7,13},{9,15},... | collective-permute-start | bytes 1572872 | tf_op jit(solution)/shard_map/ppermute | solution.py:15
  11.1 5.9 %collective-permute-start.2 = (bf16[1024,256]{0,1:T(8,128)(2,1)S(1)}, bf16[1024,256]{0,1:T(8,128)(2,1)S(1)}, u32[]{:S(2)}, u32[]{:S(2)}) collective-permute-start(bf16[1024,256]{0,1:T(8,128)(2,1)S(1)} %pad_maximum_fusion), channel_id=1, source_target_pairs={{6,0},{8,2},{10,4},{12,6},{14,8},{7,1},{9,3},{11,5},{13,7},{15,9},... | collective-permute-start | bytes 1572872 | tf_op jit(solution)/shard_map/ppermute | solution.py:15
  17.0 1.9 %collective-permute-start.1 = (bf16[1024,256]{0,1:T(8,128)(2,1)S(1)}, bf16[1024,256]{0,1:T(8,128)(2,1)S(1)}, u32[]{:S(2)}, u32[]{:S(2)}) collective-permute-start(bf16[1024,256]{0,1:T(8,128)(2,1)S(1)} %pad_maximum_fusion), channel_id=1, source_target_pairs={{4,0},{6,2},{8,4},{10,6},{12,8},{14,10},{5,1},{7,3},{9,5},{11,7},{... | collective-permute-start | bytes 1572872 | tf_op jit(solution)/shard_map/ppermute | solution.py:15
  19.0 1.6 %constant_dynamic-slice_fusion.1 = (s32[1,1]{0,1:T(1,128)}, s32[1,1]{0,1:T(1,128)}, s32[1,1]{0,1:T(1,128)}, s32[1,1]{0,1:T(1,128)}, s32[1,1]{0,1:T(1,128)}, /*index=5*/s32[1,1]{0,1:T(1,128)}) fusion(s32[8,3]{0,1:T(4,128)} %param.12, s32[]{:T(128)S(6)} %min.15, s32[]{:T(128)S(6)} %min.16, s32[]{:T(128)S(6)} %min.18, s32[]{:T(128)S(6)} %min.17), kind=kLoop, calls=%fused_computation.208 | loop fusion | bytes 64 | tf_op jit(solution)/shard_map/dynamic_slice | solution.py:21
  25.7 2.2 %collective-permute-start = (bf16[1024,256]{0,1:T(8,128)(2,1)S(1)}, bf16[1024,256]{0,1:T(8,128)(2,1)S(1)}, u32[]{:S(2)}, u32[]{:S(2)}) collective-permute-start(bf16[1024,256]{0,1:T(8,128)(2,1)S(1)} %pad_maximum_fusion), channel_id=1, source_target_pairs={{2,0},{4,2},{6,4},{8,6},{10,8},{12,10},{14,12},{3,1},{5,3},{7,5},{... | collective-permute-start | bytes 1572872 | tf_op jit(solution)/shard_map/ppermute | solution.py:15
  27.8 1.7 %multiply_reduce_fusion.1 = (f32[1024]{0:T(1024)S(1)}, f32[1024,1024]{0,1:T(8,128)S(1)}) fusion(bf16[1024,256]{0,1:T(8,128)(2,1)} %collective-permute-done.5, bf16[1024,128]{0,1:T(8,128)(2,1)S(1)} %convolution_convert_fusion.2), kind=kOutput, calls=%fused_computation.25 | convolution fusion | flops 136313856 | bytes 4460544 | tf_op jit(solution)/shard_map/qd,kd->qk/dot_general | solution.py:40
  29.5 1.7 %multiply_reduce_fusion = (f32[1024]{0:T(1024)S(1)}, f32[1024,1024]{0,1:T(8,128)S(1)}) fusion(bf16[1024,256]{0,1:T(8,128)(2,1)} %collective-permute-done.5, bf16[1024,128]{0,1:T(8,128)(2,1)S(1)} %convolution_convert_fusion.2), kind=kOutput, calls=%fused_computation.24 | convolution fusion | flops 136313856 | bytes 4460544 | tf_op jit(solution)/shard_map/qd,kd->qk/dot_general | solution.py:40
  32.7 1.7 %multiply_reduce_fusion.3 = (f32[1024]{0:T(1024)S(1)}, f32[1024,1024]{0,1:T(8,128)S(1)}) fusion(bf16[1024,256]{0,1:T(8,128)(2,1)} %collective-permute-done.4, bf16[1024,128]{0,1:T(8,128)(2,1)S(1)} %convolution_convert_fusion.2), kind=kOutput, calls=%fused_computation.27 | convolution fusion | flops 136313856 | bytes 4460544 | tf_op jit(solution)/shard_map/qd,kd->qk/dot_general | solution.py:40
  34.3 1.7 %multiply_reduce_fusion.2 = (f32[1024]{0:T(1024)S(1)}, f32[1024,1024]{0,1:T(8,128)S(1)}) fusion(bf16[1024,256]{0,1:T(8,128)(2,1)} %collective-permute-done.4, bf16[1024,128]{0,1:T(8,128)(2,1)S(1)} %convolution_convert_fusion.2), kind=kOutput, calls=%fused_computation.26 | convolution fusion | flops 136313856 | bytes 4460544 | tf_op jit(solution)/shard_map/qd,kd->qk/dot_general | solution.py:40
  37.5 3.5 %collective-permute-done.3 = bf16[1024,256]{0,1:T(8,128)(2,1)} collective-permute-done((bf16[1024,256]{0,1:T(8,128)(2,1)S(1)}, bf16[1024,256]{0,1:T(8,128)(2,1)}, u32[]{:S(2)}, u32[]{:S(2)}) %collective-permute-start.3) | collective-permute-done | bytes 524320 | tf_op jit(solution)/shard_map/ppermute | solution.py:15
  41.0 1.7 %multiply_reduce_fusion.5 = (f32[1024]{0:T(1024)S(1)}, f32[1024,1024]{0,1:T(8,128)S(1)}) fusion(bf16[1024,256]{0,1:T(8,128)(2,1)} %collective-permute-done.3, bf16[1024,128]{0,1:T(8,128)(2,1)S(1)} %convolution_convert_fusion.2), kind=kOutput, calls=%fused_computation.29 | convolution fusion | flops 136313856 | bytes 4460544 | tf_op jit(solution)/shard_map/qd,kd->qk/dot_general | solution.py:40
  43.4 1.7 %multiply_reduce_fusion.4 = (f32[1024]{0:T(1024)S(1)}, f32[1024,1024]{0,1:T(8,128)S(1)}) fusion(bf16[1024,256]{0,1:T(8,128)(2,1)} %collective-permute-done.3, bf16[1024,128]{0,1:T(8,128)(2,1)S(1)} %convolution_convert_fusion.2), kind=kOutput, calls=%fused_computation.28 | convolution fusion | flops 136313856 | bytes 4460544 | tf_op jit(solution)/shard_map/qd,kd->qk/dot_general | solution.py:40
  45.1 1.9 %fusion.29 = bf16[1024,64]{0,1:T(8,128)(2,1)S(1)} fusion(f32[1024,1024]{0,1:T(8,128)S(1)} %get-tuple-element.34, f32[1024]{0:T(1024)S(1)} %fusion.10, f32[1024]{0:T(1024)S(1)} %get-tuple-element.33, bf16[1024,256]{0,1:T(8,128)(2,1)} %collective-permute-done.5), kind=kOutput, calls=%fused_computation.71 | convolution fusion | flops 138477568 | bytes 4464640 | tf_op jit(solution)/shard_map/dot_general | solution.py:45
  46.9 1.9 %fusion.28 = bf16[1024,64]{0,1:T(8,128)(2,1)S(1)} fusion(f32[1024,1024]{0,1:T(8,128)S(1)} %get-tuple-element.32, f32[1024]{0:T(1024)S(1)} %fusion.11, f32[1024]{0:T(1024)S(1)} %get-tuple-element.31, bf16[1024,256]{0,1:T(8,128)(2,1)} %collective-permute-done.5), kind=kOutput, calls=%fused_computation.70 | convolution fusion | flops 138477568 | bytes 4464640 | tf_op jit(solution)/shard_map/dot_general | solution.py:45
  52.0 1.9 %fusion.31 = bf16[1024,64]{0,1:T(8,128)(2,1)S(1)} fusion(f32[1024,1024]{0,1:T(8,128)S(1)} %get-tuple-element.30, f32[1024]{0:T(1024)S(1)} %fusion.8, f32[1024]{0:T(1024)S(1)} %get-tuple-element.29, bf16[1024,256]{0,1:T(8,128)(2,1)} %collective-permute-done.4), kind=kOutput, calls=%fused_computation.73 | convolution fusion | flops 138477568 | bytes 4464640 | tf_op jit(solution)/shard_map/dot_general | solution.py:45
  53.9 1.9 %fusion.30 = bf16[1024,64]{0,1:T(8,128)(2,1)S(1)} fusion(f32[1024,1024]{0,1:T(8,128)S(1)} %get-tuple-element.28, f32[1024]{0:T(1024)S(1)} %fusion.9, f32[1024]{0:T(1024)S(1)} %get-tuple-element.27, bf16[1024,256]{0,1:T(8,128)(2,1)} %collective-permute-done.4), kind=kOutput, calls=%fused_computation.72 | convolution fusion | flops 138477568 | bytes 4464640 | tf_op jit(solution)/shard_map/dot_general | solution.py:45
  59.5 1.9 %fusion.33 = bf16[1024,64]{0,1:T(8,128)(2,1)S(1)} fusion(f32[1024,1024]{0,1:T(8,128)S(1)} %get-tuple-element.26, f32[1024]{0:T(1024)S(1)} %fusion.6, f32[1024]{0:T(1024)S(1)} %get-tuple-element.25, bf16[1024,256]{0,1:T(8,128)(2,1)} %collective-permute-done.3), kind=kOutput, calls=%fused_computation.75 | convolution fusion | flops 138477568 | bytes 4464640 | tf_op jit(solution)/shard_map/dot_general | solution.py:45
  61.4 1.9 %fusion.32 = bf16[1024,64]{0,1:T(8,128)(2,1)S(1)} fusion(f32[1024,1024]{0,1:T(8,128)S(1)} %get-tuple-element.24, f32[1024]{0:T(1024)S(1)} %fusion.7, f32[1024]{0:T(1024)S(1)} %get-tuple-element.23, bf16[1024,256]{0,1:T(8,128)(2,1)} %collective-permute-done.3), kind=kOutput, calls=%fused_computation.74 | convolution fusion | flops 138477568 | bytes 4464640 | tf_op jit(solution)/shard_map/dot_general | solution.py:45
  72.7 17.1 %all_to_all.16 = bf16[2,512,128]{1,2,0:T(8,128)(2,1)S(1)} all-to-all(bf16[2,512,128]{1,2,0:T(8,128)(2,1)S(1)} %add_convert_fusion), channel_id=1, replica_groups=mesh['groups'=2,'img'=4,'pair'=2,'sub'=2] {'sub'}, dimensions={0} | all-to-all | bytes 524288 | tf_op jit(solution)/shard_map/all_to_all | solution.py:90
  89.8 1.5 %fusion.183 = (f32[512]{0:T(512)S(1)}, f32[512,512]{0,1:T(8,128)S(1)}) fusion(f32[512]{0:T(512)S(1)} %copy-done.3, f32[512,512]{0,1:T(8,128)S(1)} %fusion.87, bf16[512,512]{1,0:T(8,128)(2,1)} %param.16, bf16[512,256]{0,1:T(8,128)(2,1)S(1)} %bitcast.61, bf16[256,256]{1,0:T(8,128)(2,1)S(1)} %copy-done.2), kind=kOutput, calls=%fused_computation.256 | convolution fusion | flops 202243584 | bytes 2756608 | tf_op jit(solution)/shard_map/dot_general | solution.py:96
  91.6 3.5 %fusion.27 = bf16[1,512,256]{2,1,0:T(8,128)(2,1)} fusion(bf16[512,256]{1,0:T(8,128)(2,1)S(1)} %copy-done, f32[512,512]{0,1:T(8,128)S(1)} %get-tuple-element.36, f32[512]{0:T(512)S(1)} %copy-done.4, f32[512]{0:T(512)S(1)} %copy-done.5, f32[512]{0:T(512)S(1)} %add_rsqrt_fusion, f32[512]{0:T(512)S(1)} %broadcast_multiply_fusion, f32[256]{0:T(256)S(1)} %copy-done.6, ...), kind=kOutput, calls=%fused_computation.69 | convolution fusion | flops 152829952 | bytes 1844228 | tf_op jit(solution)/shard_map/dot_general | solution.py:103
  (56 shorter events, 23.0 us)
Async XLA Ops:
  0.0 91.6 %copy-start = (bf16[512,256]{1,0:T(8,128)(2,1)S(1)}, bf16[512,256]{1,0:T(8,128)(2,1)}, u32[]{:S(2)}) copy-start(bf16[512,256]{1,0:T(8,128)(2,1)} %param.20) | copy-start | bytes 786436
  2.8 22.9 %collective-permute-start.5 = (bf16[1024,256]{0,1:T(8,128)(2,1)S(1)}, bf16[1024,256]{0,1:T(8,128)(2,1)}, u32[]{:S(2)}, u32[]{:S(2)}) collective-permute-start(bf16[1024,256]{0,1:T(8,128)(2,1)S(1)} %pad_maximum_fusion), channel_id=1, source_target_pairs={{0,2},{2,4},{4,6},{6,8},{8,10},{10,12},{12,14},{1,3},{3,5},{5,7},{... | collective-permute-start | bytes 1572872 | tf_op jit(solution)/shard_map/ppermute | solution.py:15
  5.9 26.7 %collective-permute-start.4 = (bf16[1024,256]{0,1:T(8,128)(2,1)S(1)}, bf16[1024,256]{0,1:T(8,128)(2,1)}, u32[]{:S(2)}, u32[]{:S(2)}) collective-permute-start(bf16[1024,256]{0,1:T(8,128)(2,1)S(1)} %pad_maximum_fusion), channel_id=1, source_target_pairs={{0,4},{2,6},{4,8},{6,10},{8,12},{10,14},{1,5},{3,7},{5,9},{7,11},{... | collective-permute-start | bytes 1572872 | tf_op jit(solution)/shard_map/ppermute | solution.py:15
  9.1 31.8 %collective-permute-start.3 = (bf16[1024,256]{0,1:T(8,128)(2,1)S(1)}, bf16[1024,256]{0,1:T(8,128)(2,1)}, u32[]{:S(2)}, u32[]{:S(2)}) collective-permute-start(bf16[1024,256]{0,1:T(8,128)(2,1)S(1)} %pad_maximum_fusion), channel_id=1, source_target_pairs={{0,6},{2,8},{4,10},{6,12},{8,14},{1,7},{3,9},{5,11},{7,13},{9,15},... | collective-permute-start | bytes 1572872 | tf_op jit(solution)/shard_map/ppermute | solution.py:15
  11.1 38.5 %collective-permute-start.2 = (bf16[1024,256]{0,1:T(8,128)(2,1)S(1)}, bf16[1024,256]{0,1:T(8,128)(2,1)S(1)}, u32[]{:S(2)}, u32[]{:S(2)}) collective-permute-start(bf16[1024,256]{0,1:T(8,128)(2,1)S(1)} %pad_maximum_fusion), channel_id=1, source_target_pairs={{6,0},{8,2},{10,4},{12,6},{14,8},{7,1},{9,3},{11,5},{13,7},{15,9},... | collective-permute-start | bytes 1572872 | tf_op jit(solution)/shard_map/ppermute | solution.py:15
  17.0 39.5 %collective-permute-start.1 = (bf16[1024,256]{0,1:T(8,128)(2,1)S(1)}, bf16[1024,256]{0,1:T(8,128)(2,1)S(1)}, u32[]{:S(2)}, u32[]{:S(2)}) collective-permute-start(bf16[1024,256]{0,1:T(8,128)(2,1)S(1)} %pad_maximum_fusion), channel_id=1, source_target_pairs={{4,0},{6,2},{8,4},{10,6},{12,8},{14,10},{5,1},{7,3},{9,5},{11,7},{... | collective-permute-start | bytes 1572872 | tf_op jit(solution)/shard_map/ppermute | solution.py:15
  25.7 41.5 %collective-permute-start = (bf16[1024,256]{0,1:T(8,128)(2,1)S(1)}, bf16[1024,256]{0,1:T(8,128)(2,1)S(1)}, u32[]{:S(2)}, u32[]{:S(2)}) collective-permute-start(bf16[1024,256]{0,1:T(8,128)(2,1)S(1)} %pad_maximum_fusion), channel_id=1, source_target_pairs={{2,0},{4,2},{6,4},{8,6},{10,8},{12,10},{14,12},{3,1},{5,3},{7,5},{... | collective-permute-start | bytes 1572872 | tf_op jit(solution)/shard_map/ppermute | solution.py:15
  71.4 18.5 %copy-start.2 = (bf16[256,256]{1,0:T(8,128)(2,1)S(1)}, bf16[256,256]{1,0:T(8,128)(2,1)}, u32[]{:S(2)}) copy-start(bf16[256,256]{1,0:T(8,128)(2,1)} %param.15) | copy-start | bytes 393220
  71.4 18.5 %copy-start.3 = (f32[512]{0:T(512)S(1)}, f32[512]{0:T(512)}, u32[]{:S(2)}) copy-start(f32[512]{0:T(512)} %param.17) | copy-start | bytes 6148
  72.3 19.2 %copy-start.1 = (bf16[1,1024,256]{2,1,0:T(8,128)(2,1)S(1)}, bf16[1,1024,256]{2,1,0:T(8,128)(2,1)}, u32[]{:S(2)}) copy-start(bf16[1,1024,256]{2,1,0:T(8,128)(2,1)} %param.11) | copy-start | bytes 1572868
  72.3 19.2 %copy-start.4 = (f32[512]{0:T(512)S(1)}, f32[512]{0:T(512)}, u32[]{:S(2)}) copy-start(f32[512]{0:T(512)} %param.19) | copy-start | bytes 6148
  72.4 19.2 %copy-start.5 = (f32[512]{0:T(512)S(1)}, f32[512]{0:T(512)}, u32[]{:S(2)}) copy-start(f32[512]{0:T(512)} %param.18) | copy-start | bytes 6148
  72.4 19.2 %copy-start.6 = (f32[256]{0:T(256)S(1)}, f32[256]{0:T(256)}, u32[]{:S(2)}) copy-start(f32[256]{0:T(256)} %param.21) | copy-start | bytes 3076
where the time goes:
time: 95.8 us; the launch traced here: 95.1 us
  matrix products  40.8 us (43%)
  starting transfers between devices  18.3 us (19%)
  blocking collectives  17.1 us (18%)
  other arithmetic  9.53 us (10%)
  between operations  4.11 us (4%)
  waiting for transfers between devices  3.54 us (4%)
  local copies, waits for them, and re-layouts  1.74 us (2%)
    ppermute x6, starting transfers between devices, passed_along(): return lax.ppermute(value, axis, pairs)  18.3 us
    all_to_all x1, blocking collectives, on_device(): lax.all_to_all(summed_b, 'sub', split_axis=0, concat_axis=1, tiled=True)  17.1 us
    dot_general x12, matrix products, tile_messages(): jnp.dot(row_weights, partner_values[:, lo_col:lo_col + head_width], prefe...  16.9 us
    dot_general x12, matrix products, tile_messages(): jnp.einsum('qd,kd->qk', query_part, key_part, preferred_element_type=jnp....  14.8 us
    reduce_sum x12, other arithmetic, tile_messages(): row_weights = jax.nn.softmax(scores, axis=1).astype(jnp.bfloat16)  8.99 us
    ppermute x6, waiting for transfers between devices, passed_along(): return lax.ppermute(value, axis, pairs)  3.54 us
    dot_general x1, matrix products, on_device(): jnp.dot(activated, mlp_out, preferred_element_type=jnp.float32)  3.52 us
  transfers between devices with their start and end apart: 6, of which 1 were waited for; matrix products, arithmetic and copies ran while one was open for 41% of the time, Pallas kernels for 0%

commit v1 on v0

--- a/solution.py
+++ b/solution.py
@@ -87,7 +87,10 @@
         message, unused = tile_messages(key_rows, partner_keys, partner_values)
         summed = summed + linked * message.astype(jnp.float32)
     summed_b = summed.astype(jnp.bfloat16)
-    gathered = lax.all_to_all(summed_b, "sub", split_axis=0, concat_axis=1, tiled=True)
+    peers = lax.axis_size("sub")
+    pieces = jnp.stack(jnp.split(summed_b, peers, axis=0), axis=0)
+    pieces = lax.all_to_all(pieces, "sub", split_axis=0, concat_axis=0)
+    gathered = jnp.concatenate(pieces, axis=1)
     projected = jnp.dot(gathered, out_weight, preferred_element_type=jnp.float32).astype(
         jnp.bfloat16
     )

time: 95.8 us -> 110 us (1.15)
  waiting for transfers between devices: 3.54 us -> 12.1 us
  matrix products: 40.8 us -> 48.9 us
  blocking collectives: 17.1 us -> 9.18 us
  other arithmetic: 9.53 us -> 13.7 us
  local copies, waits for them, and re-layouts: 1.74 us -> 3.12 us
    ppermute x6, waiting for transfers between devices: 3.54 us -> 12.1 us  [passed_along(): return lax.ppermute(value, axis, pairs)]
    all_to_all x1, blocking collectives: 17.1 us -> 9.18 us  [on_device(): pieces = lax.all_to_all(pieces, 'sub', split_axis=0, concat_axis=0)]
    dot_general x12, matrix products: 14.8 us -> 20.5 us  [tile_messages(): jnp.einsum('qd,kd->qk', query_part, key_part, preferred_element_type=jnp....]
    reduce_sum x12, other arithmetic: 8.99 us -> 13.1 us  [tile_messages(): row_weights = jax.nn.softmax(scores, axis=1).astype(jnp.bfloat16)]
    dot_general x12, matrix products: 16.9 us -> 19.1 us  [tile_messages(): jnp.dot(row_weights, partner_values[:, lo_col:lo_col + head_width], prefe...]
    unnamed x14 -> x20, local copies, waits for them, and re-layouts: 0.04 us -> 1.52 us
  transfers between devices with their start and end apart: 6 -> 6, of which waited for: 1 -> 3; matrix products, arithmetic and copies ran while one was open for 41% -> 21% of each run, Pallas kernels for 0% -> 0%
where the time goes in v1:
time: 110 us; the launch traced here: 109 us
  matrix products  48.9 us (44%)
  starting transfers between devices  18.3 us (17%)
  other arithmetic  13.7 us (12%)
  waiting for transfers between devices  12.1 us (11%)
  blocking collectives  9.18 us (8%)
  between operations  4.14 us (4%)
  local copies, waits for them, and re-layouts  3.12 us (3%)
    dot_general x12, matrix products, tile_messages(): jnp.einsum('qd,kd->qk', query_part, key_part, preferred_element_type=jnp....  20.5 us
    dot_general x12, matrix products, tile_messages(): jnp.dot(row_weights, partner_values[:, lo_col:lo_col + head_width], prefe...  19.1 us
    ppermute x6, starting transfers between devices, passed_along(): return lax.ppermute(value, axis, pairs)  18.3 us
    reduce_sum x12, other arithmetic, tile_messages(): row_weights = jax.nn.softmax(scores, axis=1).astype(jnp.bfloat16)  13.1 us
    ppermute x6, waiting for transfers between devices, passed_along(): return lax.ppermute(value, axis, pairs)  12.1 us
    all_to_all x1, blocking collectives, on_device(): pieces = lax.all_to_all(pieces, 'sub', split_axis=0, concat_axis=0)  9.18 us
    dot_general x1, matrix products, on_device(): jnp.dot(activated, mlp_out, preferred_element_type=jnp.float32)  3.52 us
  transfers between devices with their start and end apart: 6, of which 3 were waited for; matrix products, arithmetic and copies ran while one was open for 21% of the time, Pallas kernels for 0%

profile of v1, /device:TPU:17, one launch (start us, length us, event | category | flops | bytes accessed | tf_op | source)
XLA Modules:
  0.0 109.5 jit_solution(97318247557640523)
XLA Ops:
  2.8 3.1 %collective-permute-start.5 = (bf16[1024,256]{0,1:T(8,128)(2,1)S(1)}, bf16[1024,256]{0,1:T(8,128)(2,1)}, u32[]{:S(2)}, u32[]{:S(2)}) collective-permute-start(bf16[1024,256]{0,1:T(8,128)(2,1)S(1)} %pad_maximum_fusion), channel_id=1, source_target_pairs={{0,2},{2,4},{4,6},{6,8},{8,10},{10,12},{12,14},{1,3},{3,5},{5,7},{... | collective-permute-start | bytes 1572872 | tf_op jit(solution)/shard_map/ppermute | solution.py:15
  5.9 3.2 %collective-permute-start.4 = (bf16[1024,256]{0,1:T(8,128)(2,1)S(1)}, bf16[1024,256]{0,1:T(8,128)(2,1)}, u32[]{:S(2)}, u32[]{:S(2)}) collective-permute-start(bf16[1024,256]{0,1:T(8,128)(2,1)S(1)} %pad_maximum_fusion), channel_id=1, source_target_pairs={{0,4},{2,6},{4,8},{6,10},{8,12},{10,14},{1,5},{3,7},{5,9},{7,11},{... | collective-permute-start | bytes 1572872 | tf_op jit(solution)/shard_map/ppermute | solution.py:15
  9.1 1.9 %collective-permute-start.3 = (bf16[1024,256]{0,1:T(8,128)(2,1)S(1)}, bf16[1024,256]{0,1:T(8,128)(2,1)}, u32[]{:S(2)}, u32[]{:S(2)}) collective-permute-start(bf16[1024,256]{0,1:T(8,128)(2,1)S(1)} %pad_maximum_fusion), channel_id=1, source_target_pairs={{0,6},{2,8},{4,10},{6,12},{8,14},{1,7},{3,9},{5,11},{7,13},{9,15},... | collective-permute-start | bytes 1572872 | tf_op jit(solution)/shard_map/ppermute | solution.py:15
  11.1 6.0 %collective-permute-start.2 = (bf16[1024,256]{0,1:T(8,128)(2,1)S(1)}, bf16[1024,256]{0,1:T(8,128)(2,1)S(1)}, u32[]{:S(2)}, u32[]{:S(2)}) collective-permute-start(bf16[1024,256]{0,1:T(8,128)(2,1)S(1)} %pad_maximum_fusion), channel_id=1, source_target_pairs={{6,0},{8,2},{10,4},{12,6},{14,8},{7,1},{9,3},{11,5},{13,7},{15,9},... | collective-permute-start | bytes 1572872 | tf_op jit(solution)/shard_map/ppermute | solution.py:15
  17.1 1.9 %collective-permute-start.1 = (bf16[1024,256]{0,1:T(8,128)(2,1)S(1)}, bf16[1024,256]{0,1:T(8,128)(2,1)S(1)}, u32[]{:S(2)}, u32[]{:S(2)}) collective-permute-start(bf16[1024,256]{0,1:T(8,128)(2,1)S(1)} %pad_maximum_fusion), channel_id=1, source_target_pairs={{4,0},{6,2},{8,4},{10,6},{12,8},{14,10},{5,1},{7,3},{9,5},{11,7},{... | collective-permute-start | bytes 1572872 | tf_op jit(solution)/shard_map/ppermute | solution.py:15
  25.8 2.2 %collective-permute-start = (bf16[1024,256]{0,1:T(8,128)(2,1)S(1)}, bf16[1024,256]{0,1:T(8,128)(2,1)}, u32[]{:S(2)}, u32[]{:S(2)}) collective-permute-start(bf16[1024,256]{0,1:T(8,128)(2,1)S(1)} %pad_maximum_fusion), channel_id=1, source_target_pairs={{2,0},{4,2},{6,4},{8,6},{10,8},{12,10},{14,12},{3,1},{5,3},{7,5},{... | collective-permute-start | bytes 1572872 | tf_op jit(solution)/shard_map/ppermute | solution.py:15
  29.6 1.7 %multiply_reduce_fusion.1 = (f32[1024]{0:T(1024)S(1)}, f32[1024,1024]{0,1:T(8,128)S(1)}) fusion(bf16[1024,256]{0,1:T(8,128)(2,1)} %collective-permute-done.5, bf16[1024,128]{0,1:T(8,128)(2,1)S(1)} %convolution_convert_fusion.2), kind=kOutput, calls=%fused_computation.25 | convolution fusion | flops 136313856 | bytes 4460544 | tf_op jit(solution)/shard_map/qd,kd->qk/dot_general | solution.py:40
  32.8 1.7 %multiply_reduce_fusion.2 = (f32[1024]{0:T(1024)S(1)}, f32[1024,1024]{0,1:T(8,128)S(1)}) fusion(bf16[1024,256]{0,1:T(8,128)(2,1)} %collective-permute-done.4, bf16[1024,128]{0,1:T(8,128)(2,1)S(1)} %convolution_convert_fusion.2), kind=kOutput, calls=%fused_computation.26 | convolution fusion | flops 136313856 | bytes 4460544 | tf_op jit(solution)/shard_map/qd,kd->qk/dot_general | solution.py:40
  37.6 3.4 %collective-permute-done.3 = bf16[1024,256]{0,1:T(8,128)(2,1)} collective-permute-done((bf16[1024,256]{0,1:T(8,128)(2,1)S(1)}, bf16[1024,256]{0,1:T(8,128)(2,1)}, u32[]{:S(2)}, u32[]{:S(2)}) %collective-permute-start.3) | collective-permute-done | bytes 524320 | tf_op jit(solution)/shard_map/ppermute | solution.py:15
  52.7 8.0 %collective-permute-done = bf16[1024,256]{0,1:T(8,128)(2,1)} collective-permute-done((bf16[1024,256]{0,1:T(8,128)(2,1)S(1)}, bf16[1024,256]{0,1:T(8,128)(2,1)}, u32[]{:S(2)}, u32[]{:S(2)}) %collective-permute-start) | collective-permute-done | bytes 524320 | tf_op jit(solution)/shard_map/ppermute | solution.py:15
  60.7 3.6 %multiply_reduce_fusion.11 = (f32[1024]{0:T(1024)S(1)}, f32[1024,1024]{0,1:T(8,128)}) fusion(bf16[1024,256]{0,1:T(8,128)(2,1)} %collective-permute-done, bf16[1024,128]{0,1:T(8,128)(2,1)S(1)} %convolution_convert_fusion.2), kind=kOutput, calls=%fused_computation.35 | convolution fusion | flops 136313856 | bytes 4460544 | tf_op jit(solution)/shard_map/qd,kd->qk/dot_general | solution.py:40
  64.3 2.9 %fusion = f32[1024]{0:T(1024)S(1)} fusion(f32[1024,1024]{0,1:T(8,128)} %get-tuple-element.16, f32[1024]{0:T(1024)S(1)} %get-tuple-element.15), kind=kLoop, calls=%fused_computation.36 | loop fusion | flops 3144704 | bytes 4202496 | tf_op jit(solution)/shard_map/reduce_sum | solution.py:43
  67.2 3.6 %multiply_reduce_fusion.10 = (f32[1024]{0:T(1024)S(1)}, f32[1024,1024]{0,1:T(8,128)}) fusion(bf16[1024,256]{0,1:T(8,128)(2,1)} %collective-permute-done, bf16[1024,128]{0,1:T(8,128)(2,1)S(1)} %convolution_convert_fusion.2), kind=kOutput, calls=%fused_computation.34 | convolution fusion | flops 136313856 | bytes 4460544 | tf_op jit(solution)/shard_map/qd,kd->qk/dot_general | solution.py:40
  70.8 2.9 %fusion.1 = f32[1024]{0:T(1024)S(1)} fusion(f32[1024,1024]{0,1:T(8,128)} %get-tuple-element.14, f32[1024]{0:T(1024)S(1)} %get-tuple-element.13), kind=kLoop, calls=%fused_computation.37 | loop fusion | flops 3144704 | bytes 4202496 | tf_op jit(solution)/shard_map/reduce_sum | solution.py:43
  73.8 1.9 %fusion.28 = bf16[1024,64]{0,1:T(8,128)(2,1)S(1)} fusion(f32[1024,1024]{0,1:T(8,128)S(1)} %get-tuple-element.34, f32[1024]{0:T(1024)S(1)} %fusion.11, f32[1024]{0:T(1024)S(1)} %get-tuple-element.33, bf16[1024,256]{0,1:T(8,128)(2,1)} %collective-permute-done.5), kind=kOutput, calls=%fused_computation.70 | convolution fusion | flops 138477568 | bytes 4464640 | tf_op jit(solution)/shard_map/dot_general | solution.py:45
  75.6 1.9 %fusion.29 = bf16[1024,64]{0,1:T(8,128)(2,1)S(1)} fusion(f32[1024,1024]{0,1:T(8,128)S(1)} %get-tuple-element.36, f32[1024]{0:T(1024)S(1)} %fusion.10, f32[1024]{0:T(1024)S(1)} %get-tuple-element.35, bf16[1024,256]{0,1:T(8,128)(2,1)} %collective-permute-done.5), kind=kOutput, calls=%fused_computation.71 | convolution fusion | flops 138477568 | bytes 4464640 | tf_op jit(solution)/shard_map/dot_general | solution.py:45
  77.5 1.9 %fusion.30 = bf16[1024,64]{0,1:T(8,128)(2,1)S(1)} fusion(f32[1024,1024]{0,1:T(8,128)S(1)} %get-tuple-element.30, f32[1024]{0:T(1024)S(1)} %fusion.9, f32[1024]{0:T(1024)S(1)} %get-tuple-element.29, bf16[1024,256]{0,1:T(8,128)(2,1)} %collective-permute-done.4), kind=kOutput, calls=%fused_computation.72 | convolution fusion | flops 138477568 | bytes 4464640 | tf_op jit(solution)/shard_map/dot_general | solution.py:45
  79.3 1.9 %fusion.31 = bf16[1024,64]{0,1:T(8,128)(2,1)S(1)} fusion(f32[1024,1024]{0,1:T(8,128)S(1)} %get-tuple-element.32, f32[1024]{0:T(1024)S(1)} %fusion.8, f32[1024]{0:T(1024)S(1)} %get-tuple-element.31, bf16[1024,256]{0,1:T(8,128)(2,1)} %collective-permute-done.4), kind=kOutput, calls=%fused_computation.73 | convolution fusion | flops 138477568 | bytes 4464640 | tf_op jit(solution)/shard_map/dot_general | solution.py:45
  81.2 1.9 %fusion.32 = bf16[1024,64]{0,1:T(8,128)(2,1)S(1)} fusion(f32[1024,1024]{0,1:T(8,128)S(1)} %get-tuple-element.26, f32[1024]{0:T(1024)S(1)} %fusion.7, f32[1024]{0:T(1024)S(1)} %get-tuple-element.25, bf16[1024,256]{0,1:T(8,128)(2,1)} %collective-permute-done.3), kind=kOutput, calls=%fused_computation.74 | convolution fusion | flops 138477568 | bytes 4464640 | tf_op jit(solution)/shard_map/dot_general | solution.py:45
  83.1 1.9 %fusion.33 = bf16[1024,64]{0,1:T(8,128)(2,1)S(1)} fusion(f32[1024,1024]{0,1:T(8,128)S(1)} %get-tuple-element.28, f32[1024]{0:T(1024)S(1)} %fusion.6, f32[1024]{0:T(1024)S(1)} %get-tuple-element.27, bf16[1024,256]{0,1:T(8,128)(2,1)} %collective-permute-done.3), kind=kOutput, calls=%fused_computation.75 | convolution fusion | flops 138477568 | bytes 4464640 | tf_op jit(solution)/shard_map/dot_general | solution.py:45
  90.3 2.0 %fusion.39 = bf16[1024,64]{0,1:T(8,128)(2,1)S(1)} fusion(f32[1024,1024]{0,1:T(8,128)S(1)} %copy-done.1, f32[1024]{0:T(1024)S(1)} %fusion, f32[1024]{0:T(1024)S(1)} %get-tuple-element.15, bf16[1024,256]{0,1:T(8,128)(2,1)} %collective-permute-done), kind=kOutput, calls=%fused_computation.81 | convolution fusion | flops 138477568 | bytes 4464640 | tf_op jit(solution)/shard_map/dot_general | solution.py:45
  92.5 1.9 %fusion.38 = bf16[1024,64]{0,1:T(8,128)(2,1)S(1)} fusion(f32[1024,1024]{0,1:T(8,128)S(1)} %copy-done.2, f32[1024]{0:T(1024)S(1)} %fusion.1, f32[1024]{0:T(1024)S(1)} %get-tuple-element.13, bf16[1024,256]{0,1:T(8,128)(2,1)} %collective-permute-done), kind=kOutput, calls=%fused_computation.80 | convolution fusion | flops 138477568 | bytes 4464640 | tf_op jit(solution)/shard_map/dot_general | solution.py:45
  94.8 9.2 %all_to_all.5 = bf16[2,512,128]{1,2,0:T(8,128)(2,1)} all-to-all(bf16[2,512,128]{1,2,0:T(8,128)(2,1)S(1)} %pad_maximum_fusion.1), channel_id=1, replica_groups=mesh['groups'=2,'img'=4,'pair'=2,'sub'=2] {'sub'}, dimensions={0} | all-to-all | bytes 524288 | tf_op jit(solution)/shard_map/all_to_all | solution.py:92
  105.9 3.5 %fusion.27 = bf16[1,512,256]{2,1,0:T(8,128)(2,1)} fusion(bf16[512,256]{1,0:T(8,128)(2,1)S(1)} %copy-done, f32[512,512]{0,1:T(8,128)S(1)} %get-tuple-element.38, f32[512]{0:T(512)S(1)} %copy-done.7, f32[512]{0:T(512)S(1)} %copy-done.8, f32[512]{0:T(512)S(1)} %add_rsqrt_fusion, f32[512]{0:T(512)S(1)} %broadcast_multiply_fusion, f32[256]{0:T(256)S(1)} %copy-done.9, ...), kind=kOutput, calls=%fused_computation.69 | convolution fusion | flops 152829952 | bytes 1844228 | tf_op jit(solution)/shard_map/dot_general | solution.py:106
  (58 shorter events, 31.4 us)
Async XLA Ops:
  0.0 105.9 %copy-start = (bf16[512,256]{1,0:T(8,128)(2,1)S(1)}, bf16[512,256]{1,0:T(8,128)(2,1)}, u32[]{:S(2)}) copy-start(bf16[512,256]{1,0:T(8,128)(2,1)} %param.20) | copy-start | bytes 786436
  2.8 23.0 %collective-permute-start.5 = (bf16[1024,256]{0,1:T(8,128)(2,1)S(1)}, bf16[1024,256]{0,1:T(8,128)(2,1)}, u32[]{:S(2)}, u32[]{:S(2)}) collective-permute-start(bf16[1024,256]{0,1:T(8,128)(2,1)S(1)} %pad_maximum_fusion), channel_id=1, source_target_pairs={{0,2},{2,4},{4,6},{6,8},{8,10},{10,12},{12,14},{1,3},{3,5},{5,7},{... | collective-permute-start | bytes 1572872 | tf_op jit(solution)/shard_map/ppermute | solution.py:15
  5.9 26.8 %collective-permute-start.4 = (bf16[1024,256]{0,1:T(8,128)(2,1)S(1)}, bf16[1024,256]{0,1:T(8,128)(2,1)}, u32[]{:S(2)}, u32[]{:S(2)}) collective-permute-start(bf16[1024,256]{0,1:T(8,128)(2,1)S(1)} %pad_maximum_fusion), channel_id=1, source_target_pairs={{0,4},{2,6},{4,8},{6,10},{8,12},{10,14},{1,5},{3,7},{5,9},{7,11},{... | collective-permute-start | bytes 1572872 | tf_op jit(solution)/shard_map/ppermute | solution.py:15
  9.1 31.8 %collective-permute-start.3 = (bf16[1024,256]{0,1:T(8,128)(2,1)S(1)}, bf16[1024,256]{0,1:T(8,128)(2,1)}, u32[]{:S(2)}, u32[]{:S(2)}) collective-permute-start(bf16[1024,256]{0,1:T(8,128)(2,1)S(1)} %pad_maximum_fusion), channel_id=1, source_target_pairs={{0,6},{2,8},{4,10},{6,12},{8,14},{1,7},{3,9},{5,11},{7,13},{9,15},... | collective-permute-start | bytes 1572872 | tf_op jit(solution)/shard_map/ppermute | solution.py:15
  11.1 34.7 %collective-permute-start.2 = (bf16[1024,256]{0,1:T(8,128)(2,1)S(1)}, bf16[1024,256]{0,1:T(8,128)(2,1)S(1)}, u32[]{:S(2)}, u32[]{:S(2)}) collective-permute-start(bf16[1024,256]{0,1:T(8,128)(2,1)S(1)} %pad_maximum_fusion), channel_id=1, source_target_pairs={{6,0},{8,2},{10,4},{12,6},{14,8},{7,1},{9,3},{11,5},{13,7},{15,9},... | collective-permute-start | bytes 1572872 | tf_op jit(solution)/shard_map/ppermute | solution.py:15
  17.1 32.4 %collective-permute-start.1 = (bf16[1024,256]{0,1:T(8,128)(2,1)S(1)}, bf16[1024,256]{0,1:T(8,128)(2,1)S(1)}, u32[]{:S(2)}, u32[]{:S(2)}) collective-permute-start(bf16[1024,256]{0,1:T(8,128)(2,1)S(1)} %pad_maximum_fusion), channel_id=1, source_target_pairs={{4,0},{6,2},{8,4},{10,6},{12,8},{14,10},{5,1},{7,3},{9,5},{11,7},{... | collective-permute-start | bytes 1572872 | tf_op jit(solution)/shard_map/ppermute | solution.py:15
  25.8 34.9 %collective-permute-start = (bf16[1024,256]{0,1:T(8,128)(2,1)S(1)}, bf16[1024,256]{0,1:T(8,128)(2,1)}, u32[]{:S(2)}, u32[]{:S(2)}) collective-permute-start(bf16[1024,256]{0,1:T(8,128)(2,1)S(1)} %pad_maximum_fusion), channel_id=1, source_target_pairs={{2,0},{4,2},{6,4},{8,6},{10,8},{12,10},{14,12},{3,1},{5,3},{7,5},{... | collective-permute-start | bytes 1572872 | tf_op jit(solution)/shard_map/ppermute | solution.py:15
  45.8 1.6 %copy-start.4 = (bf16[1024,256]{0,1:T(8,128)(2,1)}, bf16[1024,256]{0,1:T(8,128)(2,1)S(1)}, u32[]{:S(2)}) copy-start(bf16[1024,256]{0,1:T(8,128)(2,1)S(1)} %collective-permute-done.2) | copy-start | bytes 1572868
  83.1 1.9 %copy-start.5 = (bf16[1024,256]{0,1:T(8,128)(2,1)S(1)}, bf16[1024,256]{0,1:T(8,128)(2,1)}, u32[]{:S(2)}) copy-start(bf16[1024,256]{0,1:T(8,128)(2,1)} %copy-done.4) | copy-start | bytes 1572868
  88.1 2.2 %copy-start.1 = (f32[1024,1024]{0,1:T(8,128)S(1)}, f32[1024,1024]{0,1:T(8,128)}, u32[]{:S(2)}) copy-start(f32[1024,1024]{0,1:T(8,128)} %get-tuple-element.16) | copy-start | bytes 12582916
  90.3 2.3 %copy-start.2 = (f32[1024,1024]{0,1:T(8,128)S(1)}, f32[1024,1024]{0,1:T(8,128)}, u32[]{:S(2)}) copy-start(f32[1024,1024]{0,1:T(8,128)} %get-tuple-element.14) | copy-start | bytes 12582916
  92.5 11.5 %copy-start.6 = (f32[512]{0:T(512)S(1)}, f32[512]{0:T(512)}, u32[]{:S(2)}) copy-start(f32[512]{0:T(512)} %param.17) | copy-start | bytes 6148
  94.4 11.5 %copy-start.3 = (bf16[1,1024,256]{2,1,0:T(8,128)(2,1)S(1)}, bf16[1,1024,256]{2,1,0:T(8,128)(2,1)}, u32[]{:S(2)}) copy-start(bf16[1,1024,256]{2,1,0:T(8,128)(2,1)} %param.11) | copy-start | bytes 1572868
  94.4 11.5 %copy-start.7 = (f32[512]{0:T(512)S(1)}, f32[512]{0:T(512)}, u32[]{:S(2)}) copy-start(f32[512]{0:T(512)} %param.19) | copy-start | bytes 6148
  94.4 11.5 %copy-start.8 = (f32[512]{0:T(512)S(1)}, f32[512]{0:T(512)}, u32[]{:S(2)}) copy-start(f32[512]{0:T(512)} %param.18) | copy-start | bytes 6148
  94.4 11.5 %copy-start.9 = (f32[256]{0:T(256)S(1)}, f32[256]{0:T(256)}, u32[]{:S(2)}) copy-start(f32[256]{0:T(256)} %param.21) | copy-start | bytes 3076
